TPU v7x, 256 devices: a whole 4x4x8 slice. The times are simulated.
256 devices in a mesh: wide: 64 (over y, z, core), narrow: 4 (over x).
Axes of the slice: x: 4, y: 4, z: 8, core: 2. Of those that a mesh axis runs over, the one named last changes fastest.
Arguments:
- diag_block: float32 [256, 512, 512], P('wide', None, 'narrow'), as said below
- panel: float32 [256, 1024, 512], P('wide', None, 'narrow'), may hold values from -2 to 2
- panel_count: int32 [256], P('wide'), may hold values from 1 to 8, 1152 in all
- pair_owner: int32 [9216, 1], P('wide'), may hold values from 0 to 63; in each aligned block of 144 rows (0 to 143, 144 to 287, ...) at most 3 rows name the same one
- pair_slot: int32 [9216], P('wide'), may hold values from 0 to 7
- ancestor: float32 [512, 128, 128], P(('wide', 'narrow')), may hold values from -6 to 6
Outputs:
- factor: float32 [256, 512, 512], P('wide', None, 'narrow')
- lower_panel: float32 [256, 1024, 512], P('wide', None, 'narrow')
- updated: float32 [512, 128, 128], P(('wide', 'narrow'))
Inputs may be any that keep to these rules, and one draw needn't show every extreme that they name: Each diag_block[s] is symmetric, and its least eigenvalue is 0.2 or more. `pair_owner`: among the rows of one index of wide no owner is named more than 3 times, a bound that some block reaches.
All inputs are finite; a program needn't handle non-finite values. No bound on the sum of `panel_count` on one device may be relied on, other than what follows from the above.
Results may differ from a plain program's by a relative error of at most 0.00016.
Values sent between devices are 32-bit elements; how exact they have to be, the bound alone decides.
A program may use at most 128 MiB of HBM per device.

v0:
```python
import jax
import jax.numpy as jnp
import numpy as np
from jax import lax
from jax.sharding import PartitionSpec as P

W = 512
B = 128
P_SIZE = 8
T_DEV = 2


def pair_lists(count):
    first = []
    second = []
    for outer in range(count):
        for inner in range(outer + 1):
            first.append(outer)
            second.append(inner)
    return (np.array(first, np.int32), np.array(second, np.int32))


def local(diag_block, panel, panel_count, pair_owner, pair_slot, ancestor):
    supers_here = diag_block.shape[0]
    col_width = diag_block.shape[2]
    narrow_index = lax.axis_index("narrow")
    narrow_count = lax.axis_size("narrow")
    wide_count = lax.axis_size("wide")
    col_start = narrow_index * col_width
    whole_diag = lax.all_gather(diag_block, "narrow", axis=2, tiled=True)
    factor = jnp.linalg.cholesky(whole_diag)
    identity = jnp.broadcast_to(jnp.eye(W, dtype=jnp.float32), factor.shape)
    inverse = lax.linalg.triangular_solve(factor, identity, left_side=True, lower=True)
    inverse_t = jnp.swapaxes(inverse, 1, 2)
    own_cols = lax.dynamic_slice_in_dim(inverse_t, col_start, col_width, 2)
    lower_panel = jnp.einsum(
        "srk,skc->src",
        lax.all_gather(panel, "narrow", axis=2, tiled=True),
        own_cols,
        precision=lax.Precision.HIGHEST,
    )
    block_index = jnp.arange(P_SIZE * B, dtype=jnp.int32) // B
    live = (block_index[None, :] < panel_count[:, None]).astype(jnp.float32)
    lower_panel = lower_panel * live[:, :, None]
    first, second = pair_lists(P_SIZE)
    blocks = lower_panel.reshape(supers_here, P_SIZE, B, col_width)
    partial_updates = jnp.einsum(
        "spac,spbc->spab", blocks[:, first], blocks[:, second], precision=lax.Precision.HIGHEST
    )
    pair_rows = supers_here * len(first)
    partial_updates = partial_updates.reshape(pair_rows, B, B)
    capacity = max(2, (pair_rows + wide_count - 1) // wide_count)
    owners = pair_owner[:, 0]
    owner_table = (owners[:, None] == jnp.arange(wide_count, dtype=jnp.int32)[None, :]).astype(
        jnp.int32
    )
    earlier = jnp.cumsum(owner_table, axis=0) - owner_table
    rank_here = jnp.sum(earlier * owner_table, axis=1)
    position = owners * capacity + rank_here
    buffer_rows = wide_count * capacity
    row_slots = T_DEV * narrow_count
    slot_ids = jnp.full((buffer_rows,), -1, jnp.int32).at[position].set(pair_slot)
    send_buffer = jnp.zeros((buffer_rows, B, B), jnp.float32).at[position].set(partial_updates)
    received, got_slots = (
        lax.all_to_all(send_buffer, "wide", split_axis=0, concat_axis=0, tiled=True),
        lax.all_to_all(slot_ids, "wide", split_axis=0, concat_axis=0, tiled=True),
    )
    slot_table = (got_slots[:, None] == jnp.arange(row_slots, dtype=jnp.int32)[None, :]).astype(
        jnp.float32
    )
    row_sums = jnp.einsum("ri,rab->iab", slot_table, received, precision=lax.Precision.HIGHEST)
    summed = lax.psum_scatter(row_sums, "narrow", scatter_dimension=0, tiled=True)
    factor_cols = lax.dynamic_slice_in_dim(factor, col_start, col_width, 2)
    return (factor_cols, lower_panel, ancestor - summed)


def solution(mesh):
    placed = (
        P("wide", None, "narrow"),
        P("wide", None, "narrow"),
        P("wide"),
        P("wide", None),
        P("wide"),
        P(("wide", "narrow"), None, None),
    )
    return jax.shard_map(
        local,
        mesh=mesh,
        in_specs=placed,
        out_specs=(
            P("wide", None, "narrow"),
            P("wide", None, "narrow"),
            P(("wide", "narrow"), None, None),
        ),
        check_vma=False,
    )
```

profile of v0, /device:TPU:8, one launch (start us, length us, event | category | flops | bytes accessed | tf_op | source)
XLA Modules:
  0.0 1013.3 jit_solution(1670821156970173186)
XLA Ops:
  13.6 12.4 %all-to-all-start = ((s32[64,3,1]{1,2,0:T(1,128)}), s32[64,3,1]{1,2,0:T(1,128)S(1)}, u32[]{:S(2)}, u32[]{:S(2)}) async-start(s32[64,3,1]{1,2,0:T(1,128)} %bitcast.20), calls=%async_computation | async-start | bytes 65536 | tf_op jit(solution)/shard_map/all_to_all | solution.py:66
  27.2 36.9 %all-gather.3.cloned.1.call-done = f32[4,512,512]{1,2,0:T(8,128)} async-done(((f32[4,512,128]{1,2,0:T(8,128)}), f32[4,512,512]{1,2,0:T(8,128)}) %all-gather.3.cloned.1.call-update) | async-done | bytes 4194320 | tf_op jit(solution)/shard_map/all_gather | solution.py:30
  64.1 5.3 copy.75
  69.4 4.5 fusion.5
  75.9 46.9 %custom-call.34 = f32[4,128,128]{2,1,0:T(8,128)S(1)} custom-call(f32[4,128,128]{2,1,0:T(8,128)S(1)} %cholesky.274), custom_call_target="Cholesky" | custom-call | tf_op jit(solution)/shard_map/jit(cholesky)/cholesky | solution.py:31
  122.8 39.3 %custom-call.35 = f32[4,1,128,128]{2,3,1,0:T(8,128)S(1)} custom-call(f32[4,1,128,128]{3,2,1,0:T(8,128)S(1)} %select_bitcast_fusion.2), custom_call_target="InvertDiagBlocksLowerTriangular" | custom-call | tf_op jit(solution)/shard_map/jit(cholesky)/cholesky | solution.py:31
  164.7 3.0 constant_dynamic-update-slice_fusion.3
  169.6 47.1 %custom-call.36 = f32[4,128,128]{2,1,0:T(8,128)S(1)} custom-call(f32[4,128,128]{2,1,0:T(8,128)S(1)} %cholesky.278), custom_call_target="Cholesky" | custom-call | tf_op jit(solution)/shard_map/jit(cholesky)/cholesky | solution.py:31
  217.6 39.3 %custom-call.37 = f32[4,1,128,128]{2,3,1,0:T(8,128)S(1)} custom-call(f32[4,1,128,128]{3,2,1,0:T(8,128)S(1)} %get-tuple-element.46), custom_call_target="InvertDiagBlocksLowerTriangular" | custom-call | tf_op jit(solution)/shard_map/jit(cholesky)/cholesky | solution.py:31
  260.9 46.9 %custom-call.38 = f32[4,128,128]{2,1,0:T(8,128)S(1)} custom-call(f32[4,128,128]{2,1,0:T(8,128)S(1)} %cholesky.283), custom_call_target="Cholesky" | custom-call | tf_op jit(solution)/shard_map/jit(cholesky)/cholesky | solution.py:31
  308.6 39.8 %custom-call.39 = f32[4,1,128,128]{2,3,1,0:T(8,128)S(1)} custom-call(f32[4,1,128,128]{3,2,1,0:T(8,128)S(1)} %get-tuple-element.44), custom_call_target="InvertDiagBlocksLowerTriangular" | custom-call | tf_op jit(solution)/shard_map/jit(cholesky)/cholesky | solution.py:31
  349.5 2.6 convolution_subtract_fusion.3
  352.1 46.9 %custom-call.40 = f32[4,128,128]{2,1,0:T(8,128)S(1)} custom-call(f32[4,128,128]{2,1,0:T(8,128)S(1)} %convolution_subtract_fusion.3), custom_call_target="Cholesky" | custom-call | tf_op jit(solution)/shard_map/jit(cholesky)/cholesky | solution.py:31
  400.2 6.7 broadcast_select_fusion
  406.9 15.0 %while.1 = (s32[]{:T(128)}, f32[4,512,512]{2,1,0:T(8,128)}, s32[4,2]{0,1:T(2,128)S(1)}, f32[4,4,128,128]{3,2,0,1:T(8,128)}, s32[]{:T(128)}) while((s32[]{:T(128)}, f32[4,512,512]{2,1,0:T(8,128)}, s32[4,2]{0,1:T(2,128)S(1)}, f32[4,4,128,128]{3,2,0,1:T(8,128)}, s32[]{:T(128)}) %tuple.40), condition=%wide.while_cond, body=%wide.while_body.sunk | while | flops 2 | bytes 525421 | solution.py:33
  407.5 3.2 bitcast_dynamic-update-slice_fusion.2
  411.3 3.2 bitcast_dynamic-update-slice_fusion.2
  415.1 3.2 bitcast_dynamic-update-slice_fusion.2
  418.9 3.1 bitcast_dynamic-update-slice_fusion.2
  421.9 158.2 %custom-call.41 = f32[4,4,128,128]{2,3,1,0:T(8,128)S(1)} custom-call(f32[4,4,128,128]{3,2,1,0:T(8,128)} %bitcast.100), custom_call_target="InvertDiagBlocksLowerTriangular" | custom-call | tf_op jit(solution)/shard_map/triangular_solve | solution.py:33
  588.7 3.3 fusion.16
  592.0 3.1 fusion.37
  595.1 13.3 %multiply_bitcast_fusion = f32[4,1024,128]{1,2,0:T(8,128)} fusion(f32[4,1024,512]{2,1,0:T(8,128)} %all-gather.5.cloned.1.call-done, s32[]{:T(128)S(6)} %select_n.29, f32[4,128,512]{2,1,0:T(8,128)S(1)} %fusion.35, f32[4,128,512]{2,1,0:T(8,128)S(1)} %fusion.40, f32[4,128,512]{2,1,0:T(8,128)S(1)} %fusion.38, f32[4,128,512]{2,1,0:T(8,128)} %fusion.37, ...), kind=kOutput, calls=%fused_computation.28 | convolution fusion | flops 3222536192 | bytes 14696452 | tf_op jit(solution)/shard_map/srk,skc->src/dot_general | solution.py:36
  610.3 6.7 gather_fusion.1
  617.1 6.7 gather_fusion
  623.8 25.8 %fusion.2 = f32[4,36,128,128]{3,2,1,0:T(8,128)} fusion(f32[36,4,128,128]{3,2,1,0:T(8,128)} %gather_fusion.1, f32[36,4,128,128]{3,2,1,0:T(8,128)} %gather_fusion), kind=kOutput, calls=%fused_computation.8 | convolution fusion | flops 3623878656 | bytes 28311552 | tf_op jit(solution)/shard_map/spac,spbc->spab/dot_general | solution.py:47
  649.6 6.2 broadcast_in_dim.43
  655.7 26.3 %scatter_fusion = f32[192,128,128]{2,1,0:T(8,128)} fusion(f32[192,128,128]{2,1,0:T(8,128)} %broadcast_in_dim.43, s32[144]{0:T(256)S(1)} %bitcast.98, f32[144,128,128]{2,1,0:T(8,128)} %bitcast.94), kind=kCustom, calls=%fused_computation.3 | custom fusion | bytes 28312128 | tf_op jit(solution)/shard_map/scatter | solution.py:63
  682.1 10.7 %all-to-all-start.1 = ((f32[192,128,128]{2,1,0:T(8,128)}), f32[192,128,128]{2,1,0:T(8,128)}, u32[]{:S(2)}, u32[]{:S(2)}) async-start(f32[192,128,128]{2,1,0:T(8,128)} %scatter_fusion), calls=%async_computation.1 | async-start | bytes 25165824 | tf_op jit(solution)/shard_map/all_to_all | solution.py:65
  694.2 273.1 %all-to-all-done.1 = f32[192,128,128]{2,1,0:T(8,128)} async-done(((f32[192,128,128]{2,1,0:T(8,128)}), f32[192,128,128]{2,1,0:T(8,128)}, u32[]{:S(2)}, u32[]{:S(2)}) %all-to-all-start.1) | async-done | bytes 12582944 | tf_op jit(solution)/shard_map/all_to_all | solution.py:65
  967.4 15.5 %fusion = f32[8,128,128]{2,0,1:T(8,128)S(1)} fusion(f32[192,128,128]{2,1,0:T(8,128)} %all-to-all-done.1, s32[192]{0:T(256)S(1)} %eq.54), kind=kOutput, calls=%fused_computation.6 | convolution fusion | flops 301991424 | bytes 13107968 | tf_op jit(solution)/shard_map/ri,rab->iab/dot_general | solution.py:71
  986.0 18.7 %reduce-scatter.2.cloned.1.call-done = f32[2,128,128]{2,1,0:T(8,128)} async-done(((f32[8,128,128]{2,1,0:T(8,128)}), f32[2,128,128]{2,1,0:T(8,128)}) %reduce-scatter.2.cloned.1.call-update) | async-done | bytes 131088 | tf_op jit(solution)/shard_map/reduce_scatter | solution.py:72
  (83 shorter events, 40.9 us)
Async XLA Ops:
  7.2 18.9 %copy-start.6 = (s32[36]{0:T(128)S(1)}, s32[36]{0:T(128)}, u32[]{:S(2)}) copy-start(s32[36]{0:T(128)} %constant.237) | copy-start | bytes 436
  7.2 18.9 %copy-start.5 = (s32[36]{0:T(128)S(1)}, s32[36]{0:T(128)}, u32[]{:S(2)}) copy-start(s32[36]{0:T(128)} %constant.238) | copy-start | bytes 436
  7.2 3.4 copy-start.4
  7.2 19.1 %copy-start.7 = (s32[4]{0:T(128)S(1)}, s32[4]{0:T(128)}, u32[]{:S(2)}) copy-start(s32[4]{0:T(128)} %param.12) | copy-start | bytes 52
  7.2 56.9 %all-gather.3.cloned.1.call-start = ((), (), s32[]{:S(2)}) async-start(), calls=%async_computation.3 | async-start | bytes 5242880 | tf_op jit(solution)/shard_map/all_gather | solution.py:30
  9.8 585.3 %all-gather.5.cloned.1.call-start = ((), (), s32[]{:S(2)}) async-start(), calls=%async_computation.4 | async-start | bytes 10485760 | tf_op jit(solution)/shard_map/all_gather | solution.py:38
  13.6 668.5 %all-to-all-start = ((s32[64,3,1]{1,2,0:T(1,128)}), s32[64,3,1]{1,2,0:T(1,128)S(1)}, u32[]{:S(2)}, u32[]{:S(2)}) async-start(s32[64,3,1]{1,2,0:T(1,128)} %bitcast.20), calls=%async_computation | async-start | bytes 65536 | tf_op jit(solution)/shard_map/all_to_all | solution.py:66
  73.9 2.0 copy-start.1
  580.1 4.1 copy-start.2
  610.3 6.8 copy-start
  682.1 285.3 %all-to-all-start.1 = ((f32[192,128,128]{2,1,0:T(8,128)}), f32[192,128,128]{2,1,0:T(8,128)}, u32[]{:S(2)}, u32[]{:S(2)}) async-start(f32[192,128,128]{2,1,0:T(8,128)} %scatter_fusion), calls=%async_computation.1 | async-start | bytes 25165824 | tf_op jit(solution)/shard_map/all_to_all | solution.py:65
  692.8 311.9 %reduce-scatter.2.cloned.1.call-start = ((), (), s32[]{:S(2)}) async-start(), calls=%async_computation.5 | async-start | bytes 655360 | tf_op jit(solution)/shard_map/reduce_scatter | solution.py:72
  694.2 310.5 %copy-start.3 = (f32[2,128,128]{2,1,0:T(8,128)S(1)}, f32[2,128,128]{2,1,0:T(8,128)}, u32[]{:S(2)}) copy-start(f32[2,128,128]{2,1,0:T(8,128)} %param.15) | copy-start | bytes 393220
Sparse Core Ops, SparseCore 0:
  10.4 53.6 all-gather.2
  65.9 90.4 all-gather.4
  983.9 20.7 reduce-scatter.1
where the time goes:
time: 1020 us; the launch traced here: 1010 us
  other arithmetic  482 us (47%)
  waiting for transfers between devices  329 us (32%)
  matrix products  82.2 us (8%)
  local copies, waits for them, and re-layouts  82 us (8%)
  starting transfers between devices  23.3 us (2%)
  between operations  14.6 us (1%)
    another operation x16, other arithmetic, local(): factor = jnp.linalg.cholesky(whole_diag)  309 us
    all_to_all x1, waiting for transfers between devices, local(): lax.all_to_all(send_buffer, 'wide', split_axis=0, concat_axis=0, tiled=True)  273 us
    another operation x3, other arithmetic, local(): lax.linalg.triangular_solve(factor, identity, left_side=True, lower=True)  165 us
    all_gather x1, waiting for transfers between devices, local(): whole_diag = lax.all_gather(diag_block, 'narrow', axis=2, tiled=True)  36.9 us
    scatter x1, local copies, waits for them, and re-layouts, local(): jnp.zeros((buffer_rows, B, B), jnp.float32).at[position]  26.3 us
    dot_general x1, matrix products, local(): jnp.einsum('spac,spbc->spab', blocks[:, first], blocks[:, second], precis...  25.8 us
  transfers between devices with their start and end apart: 5, of which 3 were waited for; matrix products, arithmetic and copies ran while one was open for 61% of the time, Pallas kernels for 0%

commit v1 on v0

--- a/solution.py
+++ b/solution.py
@@ -27,7 +27,9 @@
     narrow_count = lax.axis_size("narrow")
     wide_count = lax.axis_size("wide")
     col_start = narrow_index * col_width
-    whole_diag = lax.all_gather(diag_block, "narrow", axis=2, tiled=True)
+    whole_diag = jnp.concatenate(
+        lax.all_to_all(jnp.stack([diag_block] * lax.axis_size("narrow")), "narrow", 0, 0), axis=2
+    )
     factor = jnp.linalg.cholesky(whole_diag)
     identity = jnp.broadcast_to(jnp.eye(W, dtype=jnp.float32), factor.shape)
     inverse = lax.linalg.triangular_solve(factor, identity, left_side=True, lower=True)

time: 1020 us -> 1070 us (1.049)
  waiting for transfers between devices: 329 us -> 370 us
    all_to_all x0 -> x1, waiting for transfers between devices: none -> 74.9 us  [local(): lax.all_to_all(jnp.stack([diag_block] * lax.axis_size('narrow')), 'narrow...]
    all_gather x1 -> x0, waiting for transfers between devices: 36.9 us -> none  [local(): whole_diag = lax.all_gather(diag_block, 'narrow', axis=2, tiled=True)]
  transfers between devices with their start and end apart: 5 -> 5, of which waited for: 3 -> 3; matrix products, arithmetic and copies ran while one was open for 61% -> 59% of each run, Pallas kernels for 0% -> 0%
where the time goes in v1:
time: 1070 us
  other arithmetic  482 us (45%)
  waiting for transfers between devices  370 us (35%)
  local copies, waits for them, and re-layouts  88.5 us (8%)
  matrix products  82.2 us (8%)
  starting transfers between devices  29.7 us (3%)
  between operations  14.8 us (1%)
    another operation x16, other arithmetic, local(): factor = jnp.linalg.cholesky(whole_diag)  309 us
    all_to_all x1, waiting for transfers between devices, local(): lax.all_to_all(send_buffer, 'wide', split_axis=0, concat_axis=0, tiled=True)  273 us
    another operation x3, other arithmetic, local(): lax.linalg.triangular_solve(factor, identity, left_side=True, lower=True)  165 us
    all_to_all x1, waiting for transfers between devices, local(): lax.all_to_all(jnp.stack([diag_block] * lax.axis_size('narrow')), 'narrow...  74.9 us
    scatter x1, local copies, waits for them, and re-layouts, local(): jnp.zeros((buffer_rows, B, B), jnp.float32).at[position]  26.3 us
    dot_general x1, matrix products, local(): jnp.einsum('spac,spbc->spab', blocks[:, first], blocks[:, second], precis...  25.8 us
  transfers between devices with their start and end apart: 5, of which 3 were waited for; matrix products, arithmetic and copies ran while one was open for 59% of the time, Pallas kernels for 0%

profile of v1, /device:TPU:8, one launch (start us, length us, event | category | flops | bytes accessed | tf_op | source)
XLA Modules:
  0.0 1067.0 jit_solution(18202277091695760639)
XLA Ops:
  12.0 5.1 all-to-all-start
  21.3 74.9 %all-to-all-done = f32[4,4,512,128]{2,3,1,0:T(8,128)} async-done(((f32[4,4,512,128]{2,3,1,0:T(8,128)}), f32[4,4,512,128]{2,3,1,0:T(8,128)}, u32[]{:S(2)}, u32[]{:S(2)}) %all-to-all-start) | async-done | bytes 4194336 | tf_op jit(solution)/shard_map/all_to_all | solution.py:31
  96.2 14.0 %all-to-all-start.1 = ((s32[64,3,1]{1,2,0:T(1,128)}), s32[64,3,1]{1,2,0:T(1,128)S(1)}, u32[]{:S(2)}, u32[]{:S(2)}) async-start(s32[64,3,1]{1,2,0:T(1,128)} %bitcast.22), calls=%async_computation.1 | async-start | bytes 65536 | tf_op jit(solution)/shard_map/all_to_all | solution.py:68
  110.2 4.8 copy.76
  114.9 5.3 copy.77
  120.2 4.6 fusion.5
  126.9 46.9 %custom-call.34 = f32[4,128,128]{2,1,0:T(8,128)S(1)} custom-call(f32[4,128,128]{2,1,0:T(8,128)S(1)} %cholesky.274), custom_call_target="Cholesky" | custom-call | tf_op jit(solution)/shard_map/jit(cholesky)/cholesky | solution.py:33
  173.8 39.3 %custom-call.35 = f32[4,1,128,128]{2,3,1,0:T(8,128)S(1)} custom-call(f32[4,1,128,128]{3,2,1,0:T(8,128)S(1)} %select_bitcast_fusion.2), custom_call_target="InvertDiagBlocksLowerTriangular" | custom-call | tf_op jit(solution)/shard_map/jit(cholesky)/cholesky | solution.py:33
  220.6 47.1 %custom-call.36 = f32[4,128,128]{2,1,0:T(8,128)S(1)} custom-call(f32[4,128,128]{2,1,0:T(8,128)S(1)} %cholesky.278), custom_call_target="Cholesky" | custom-call | tf_op jit(solution)/shard_map/jit(cholesky)/cholesky | solution.py:33
  268.5 39.3 %custom-call.37 = f32[4,1,128,128]{2,3,1,0:T(8,128)S(1)} custom-call(f32[4,1,128,128]{3,2,1,0:T(8,128)S(1)} %get-tuple-element.46), custom_call_target="InvertDiagBlocksLowerTriangular" | custom-call | tf_op jit(solution)/shard_map/jit(cholesky)/cholesky | solution.py:33
  311.9 46.9 %custom-call.38 = f32[4,128,128]{2,1,0:T(8,128)S(1)} custom-call(f32[4,128,128]{2,1,0:T(8,128)S(1)} %cholesky.283), custom_call_target="Cholesky" | custom-call | tf_op jit(solution)/shard_map/jit(cholesky)/cholesky | solution.py:33
  359.5 39.8 %custom-call.39 = f32[4,1,128,128]{2,3,1,0:T(8,128)S(1)} custom-call(f32[4,1,128,128]{3,2,1,0:T(8,128)S(1)} %get-tuple-element.44), custom_call_target="InvertDiagBlocksLowerTriangular" | custom-call | tf_op jit(solution)/shard_map/jit(cholesky)/cholesky | solution.py:33
  403.1 46.9 %custom-call.40 = f32[4,128,128]{2,1,0:T(8,128)S(1)} custom-call(f32[4,128,128]{2,1,0:T(8,128)S(1)} %convolution_subtract_fusion.3), custom_call_target="Cholesky" | custom-call | tf_op jit(solution)/shard_map/jit(cholesky)/cholesky | solution.py:33
  451.1 6.7 broadcast_select_fusion
  457.8 15.3 %while.1 = (s32[]{:T(128)}, f32[4,512,512]{2,1,0:T(8,128)}, s32[4,2]{0,1:T(2,128)S(1)}, f32[4,4,128,128]{3,2,0,1:T(8,128)}, s32[]{:T(128)}) while((s32[]{:T(128)}, f32[4,512,512]{2,1,0:T(8,128)}, s32[4,2]{0,1:T(2,128)S(1)}, f32[4,4,128,128]{3,2,0,1:T(8,128)}, s32[]{:T(128)}) %tuple.40), condition=%wide.while_cond, body=%wide.while_body.sunk | while | flops 2 | bytes 525421 | solution.py:35
  458.5 3.2 bitcast_dynamic-update-slice_fusion.2
  462.4 3.2 bitcast_dynamic-update-slice_fusion.2
  466.2 3.2 bitcast_dynamic-update-slice_fusion.2
  470.1 3.1 bitcast_dynamic-update-slice_fusion.2
  473.1 158.2 %custom-call.41 = f32[4,4,128,128]{2,3,1,0:T(8,128)S(1)} custom-call(f32[4,4,128,128]{3,2,1,0:T(8,128)} %bitcast.104), custom_call_target="InvertDiagBlocksLowerTriangular" | custom-call | tf_op jit(solution)/shard_map/triangular_solve | solution.py:35
  639.9 3.3 fusion.16
  643.2 3.1 fusion.37
  646.3 13.3 %multiply_bitcast_fusion = f32[4,1024,128]{1,2,0:T(8,128)} fusion(f32[4,1024,512]{2,1,0:T(8,128)} %all-gather.2.cloned.1.call-done, s32[]{:T(128)S(6)} %select_n.29, f32[4,128,512]{2,1,0:T(8,128)S(1)} %fusion.35, f32[4,128,512]{2,1,0:T(8,128)S(1)} %fusion.40, f32[4,128,512]{2,1,0:T(8,128)S(1)} %fusion.38, f32[4,128,512]{2,1,0:T(8,128)} %fusion.37, ...), kind=kOutput, calls=%fused_computation.28 | convolution fusion | flops 3222536192 | bytes 14696452 | tf_op jit(solution)/shard_map/srk,skc->src/dot_general | solution.py:38
  661.5 6.7 gather_fusion.1
  668.3 6.7 gather_fusion
  675.0 25.8 %fusion.2 = f32[4,36,128,128]{3,2,1,0:T(8,128)} fusion(f32[36,4,128,128]{3,2,1,0:T(8,128)} %gather_fusion.1, f32[36,4,128,128]{3,2,1,0:T(8,128)} %gather_fusion), kind=kOutput, calls=%fused_computation.8 | convolution fusion | flops 3623878656 | bytes 28311552 | tf_op jit(solution)/shard_map/spac,spbc->spab/dot_general | solution.py:49
  700.8 6.2 broadcast_in_dim.43
  706.9 26.3 %scatter_fusion = f32[192,128,128]{2,1,0:T(8,128)} fusion(f32[192,128,128]{2,1,0:T(8,128)} %broadcast_in_dim.43, s32[144]{0:T(256)S(1)} %bitcast.102, f32[144,128,128]{2,1,0:T(8,128)} %bitcast.98), kind=kCustom, calls=%fused_computation.3 | custom fusion | bytes 28312128 | tf_op jit(solution)/shard_map/scatter | solution.py:65
  733.3 10.5 all-to-all-start.2
  745.2 273.1 %all-to-all-done.2 = f32[192,128,128]{2,1,0:T(8,128)} async-done(((f32[192,128,128]{2,1,0:T(8,128)}), f32[192,128,128]{2,1,0:T(8,128)}, u32[]{:S(2)}, u32[]{:S(2)}) %all-to-all-start.2) | async-done | bytes 12582944 | tf_op jit(solution)/shard_map/all_to_all | solution.py:67
  1018.4 15.5 %fusion = f32[8,128,128]{2,0,1:T(8,128)S(1)} fusion(f32[192,128,128]{2,1,0:T(8,128)} %all-to-all-done.2, s32[192]{0:T(256)S(1)} %eq.54), kind=kOutput, calls=%fused_computation.6 | convolution fusion | flops 301991424 | bytes 13107968 | tf_op jit(solution)/shard_map/ri,rab->iab/dot_general | solution.py:73
  1037.0 21.2 %reduce-scatter.2.cloned.1.call-done = f32[2,128,128]{2,1,0:T(8,128)} async-done(((f32[8,128,128]{2,1,0:T(8,128)}), f32[2,128,128]{2,1,0:T(8,128)}) %reduce-scatter.2.cloned.1.call-update) | async-done | bytes 131088 | tf_op jit(solution)/shard_map/reduce_scatter | solution.py:74
  (84 shorter events, 48.1 us)
Async XLA Ops:
  7.2 639.2 %all-gather.2.cloned.1.call-start = ((), (), s32[]{:S(2)}) async-start(), calls=%async_computation.4 | async-start | bytes 10485760 | tf_op jit(solution)/shard_map/all_gather | solution.py:40
  12.0 5.1 copy-start.4
  12.0 8.1 copy-start.6
  12.0 8.1 copy-start.5
  12.0 8.4 copy-start.7
  12.0 84.2 %all-to-all-start = ((f32[4,4,512,128]{2,3,1,0:T(8,128)}), f32[4,4,512,128]{2,3,1,0:T(8,128)}, u32[]{:S(2)}, u32[]{:S(2)}) async-start(f32[4,4,512,128]{2,3,1,0:T(8,128)} %stack.2), calls=%async_computation | async-start | bytes 8388608 | tf_op jit(solution)/shard_map/all_to_all | solution.py:31
  96.2 637.1 %all-to-all-start.1 = ((s32[64,3,1]{1,2,0:T(1,128)}), s32[64,3,1]{1,2,0:T(1,128)S(1)}, u32[]{:S(2)}, u32[]{:S(2)}) async-start(s32[64,3,1]{1,2,0:T(1,128)} %bitcast.22), calls=%async_computation.1 | async-start | bytes 65536 | tf_op jit(solution)/shard_map/all_to_all | solution.py:68
  124.8 2.0 copy-start.1
  631.3 4.1 copy-start.2
  661.5 6.8 copy-start
  733.3 285.1 %all-to-all-start.2 = ((f32[192,128,128]{2,1,0:T(8,128)}), f32[192,128,128]{2,1,0:T(8,128)}, u32[]{:S(2)}, u32[]{:S(2)}) async-start(f32[192,128,128]{2,1,0:T(8,128)} %scatter_fusion), calls=%async_computation.2 | async-start | bytes 25165824 | tf_op jit(solution)/shard_map/all_to_all | solution.py:67
  743.8 314.4 %reduce-scatter.2.cloned.1.call-start = ((), (), s32[]{:S(2)}) async-start(), calls=%async_computation.5 | async-start | bytes 655360 | tf_op jit(solution)/shard_map/reduce_scatter | solution.py:74
  745.2 313.0 %copy-start.3 = (f32[2,128,128]{2,1,0:T(8,128)S(1)}, f32[2,128,128]{2,1,0:T(8,128)}, u32[]{:S(2)}) copy-start(f32[2,128,128]{2,1,0:T(8,128)} %param.15) | copy-start | bytes 393220
Sparse Core Ops, SparseCore 0:
  9.8 127.4 all-gather.1
  1034.9 23.2 reduce-scatter.1
